TPU v7x, 512 devices: a whole 4x4x16 slice. The times are simulated.
512 devices in a mesh: pipe: 8 (over y_lo, x), dp: 64 (over z, y_hi, core).
Axes of the slice: x: 4, y: 4 (y_hi: 2, y_lo: 2; y = y_hi * 2 + y_lo), z: 16, core: 2. Of those that a mesh axis runs over, the one named last changes fastest.
Arguments:
- visual_fragments: bfloat16 [8, 64, 64, 1152], P(None, 'dp'), may hold values from -6 to 6
- widening_kernel: bfloat16 [8, 1152, 2176], P('pipe', None, 'dp'), may hold values from -0.1875 to 0.1875
- narrowing_kernel: bfloat16 [8, 2176, 1152], P('pipe', 'dp'), may hold values from -0.125 to 0.125
- caption_outputs: bfloat16 [4608, 1152], P(('pipe', 'dp')), may hold values from -6 to 6
- earlier_averaged: float32 [4096, 1152], P(('pipe', 'dp')), may hold values from -6 to 6
- match_targets: int32 [4608], replicated, may hold values from 0 to 4607, each once
- score_scaling: float32 [1], replicated, may hold values from 5 to 15
- score_shift: float32 [1], replicated, may hold values from -4 to -2
Outputs:
- image_grad: float32 [4608, 1152], P(('pipe', 'dp'))
- text_grad: float32 [4608, 1152], P(('pipe', 'dp'))
Inputs may be any that keep to these rules, and one draw needn't show every extreme that they name: match_targets is a permutation: every text is the positive of exactly one image.
All inputs are finite; a program needn't handle non-finite values.
Results may differ from a plain program's by a relative error of at most 0.017.
Values may be sent and summed in bfloat16 or wider, within the bound.
No kernel may reach another device: no remote copies, remote signals or barrier semaphores. Data moves between devices by JAX's collectives and lax.ppermute only.
A program may use at most 128 MiB of HBM per device.

v0:
```python
import jax
import jax.numpy as jnp
from jax import lax
from jax.sharding import PartitionSpec as P


def from_behind(value, axis, steps):
    count = lax.axis_size(axis)
    pairs = [(source, (source + steps) % count) for source in range(count)]
    return lax.ppermute(value, axis, pairs)


def layer_norm(hidden_rows):
    values = hidden_rows.astype(jnp.float32)
    centre = jnp.mean(values, axis=-1, keepdims=True)
    shifted = values - centre
    variance = jnp.mean(shifted * shifted, axis=-1, keepdims=True)
    return (shifted * lax.rsqrt(variance + 1e-06)).astype(jnp.bfloat16)


def section_block(hidden_rows, w_up, w_down):
    normed = layer_norm(hidden_rows)
    pre_act = jnp.dot(normed, w_up, preferred_element_type=jnp.float32)
    activated = jax.nn.gelu(pre_act, approximate=True).astype(jnp.bfloat16)
    updated = hidden_rows.astype(jnp.float32) + jnp.dot(
        activated, w_down, preferred_element_type=jnp.float32
    )
    return updated.astype(jnp.bfloat16)


def unit_rows(values):
    values = values.astype(jnp.float32)
    total = jnp.sum(values * values, axis=-1, keepdims=True)
    return (values * lax.rsqrt(total + 1e-06)).astype(jnp.bfloat16)


def coupling_factors(
    picture_group, source_caption_tile, match_entries, target_tile, sharpness_factor, shift_addend
):
    similarity_scores = (
        sharpness_factor
        * jnp.dot(picture_group, source_caption_tile.T, preferred_element_type=jnp.float32)
        + shift_addend
    )
    matching_couples = match_entries[:, None] == target_tile[None, :]
    coefficient_grid = jnp.where(
        matching_couples,
        -sharpness_factor * jax.nn.sigmoid(-similarity_scores),
        sharpness_factor * jax.nn.sigmoid(similarity_scores),
    )
    return coefficient_grid.astype(jnp.bfloat16)


def body(
    visual_fragments,
    widening_kernel,
    narrowing_kernel,
    caption_outputs,
    earlier_averaged,
    match_targets,
    score_scaling,
    score_shift,
):
    sections = lax.axis_size("pipe")
    section_id = lax.axis_index("pipe")
    data_count = lax.axis_size("dp")
    data_id = lax.axis_index("dp")
    micros, img_mb, patch_count, model_width = visual_fragments.shape
    tok_rows = img_mb * patch_count
    sharpness_factor = score_scaling[0]
    shift_addend = score_shift[0]
    caption_vectors = unit_rows(caption_outputs)
    up_full, down_full = (
        lax.all_gather(widening_kernel, "dp", axis=2, tiled=True),
        lax.all_gather(narrowing_kernel, "dp", axis=1, tiled=True),
    )
    up_full = up_full[0]
    down_full = down_full[0]
    panels = visual_fragments.reshape(micros, tok_rows, model_width)

    def advance(step, current):
        pick = jnp.clip(sections - 1 - step, 0, micros - 1)
        incoming = lax.dynamic_index_in_dim(panels, pick, 0, keepdims=False)
        current = jnp.where((section_id == 0) & (step < sections), incoming, current)
        active = (step >= section_id) & (step - section_id < sections)
        current = lax.cond(
            active,
            lambda carried: section_block(carried, up_full, down_full),
            lambda carried: carried,
            current,
        )
        return from_behind(current, "pipe", 1)

    finished = lax.fori_loop(
        0, 2 * sections - 1, advance, jnp.zeros((tok_rows, model_width), jnp.bfloat16)
    )
    pooled = jnp.mean(
        finished.astype(jnp.float32).reshape(img_mb, patch_count, model_width), axis=1
    )
    picture_vectors = jnp.concatenate([unit_rows(pooled), unit_rows(earlier_averaged)], axis=0)
    rows_dev = picture_vectors.shape[0]
    row_width = data_count * rows_dev
    text_row_block = lax.all_gather(caption_vectors, "dp", axis=0, tiled=True)
    image_column_block = lax.all_gather(picture_vectors, "pipe", axis=0, tiled=True)
    label_table = match_targets.reshape(sections, row_width)
    label_columns = lax.dynamic_slice_in_dim(label_table, data_id * rows_dev, rows_dev, 1).reshape(
        -1
    )
    column_text_block = section_id * row_width + jnp.arange(row_width, dtype=jnp.int32)
    grid_weights = coupling_factors(
        image_column_block,
        text_row_block,
        label_columns,
        column_text_block,
        sharpness_factor,
        shift_addend,
    )
    block = grid_weights
    image_grad = lax.psum_scatter(
        jnp.dot(block, text_row_block, preferred_element_type=jnp.float32).astype(jnp.bfloat16),
        "pipe",
        scatter_dimension=0,
        tiled=True,
    ).astype(jnp.float32)
    block = grid_weights
    text_grad = lax.psum_scatter(
        jnp.dot(block.T, image_column_block, preferred_element_type=jnp.float32),
        "dp",
        scatter_dimension=0,
        tiled=True,
    )
    return (image_grad, text_grad)


def solution(mesh):
    placed = (
        P(None, "dp", None, None),
        P("pipe", None, "dp"),
        P("pipe", "dp", None),
        P(("pipe", "dp"), None),
        P(("pipe", "dp"), None),
        P(),
        P(),
        P(),
    )
    return jax.shard_map(
        body,
        mesh=mesh,
        in_specs=placed,
        out_specs=(P(("pipe", "dp"), None), P(("pipe", "dp"), None)),
        check_vma=False,
    )
```

profile of v0, /device:TPU:1, one launch (start us, length us, event | category | flops | bytes accessed | tf_op | source)
XLA Modules:
  0.0 1396.2 jit_solution(13821860944951176592)
XLA Ops:
  17.2 145.3 %all-gather.10.cloned.1.call-done = bf16[64,9,1152]{2,1,0:T(8,128)(2,1)} async-done(((bf16[1,9,1152]{2,1,0:T(8,128)(2,1)}), bf16[64,9,1152]{2,1,0:T(8,128)(2,1)}) %all-gather.10.cloned.1.call-update) | async-done | bytes 1327120 | tf_op jit(solution)/shard_map/all_gather | solution.py:103
  162.5 2.6 reshape.79
  165.1 165.6 %all-gather.8.cloned.1.call-done = bf16[1,2176,1152]{2,0,1:T(2,128)(2,1)} async-done(((bf16[1,34,1152]{2,0,1:T(2,128)(2,1)}), bf16[1,2176,1152]{2,0,1:T(2,128)(2,1)}) %all-gather.8.cloned.1.call-update) | async-done | bytes 5013520 | tf_op jit(solution)/shard_map/all_gather | solution.py:75
  330.7 6.9 copy.20
  337.6 161.9 %all-gather.6.cloned.1.call-done = bf16[1,1152,2176]{1,0,2:T(2,128)(2,1)} async-done(((bf16[1,1152,34]{1,0,2:T(2,128)(2,1)}), bf16[1,1152,2176]{1,0,2:T(2,128)(2,1)}) %all-gather.6.cloned.1.call-update) | async-done | bytes 5013520 | tf_op jit(solution)/shard_map/all_gather | solution.py:74
  499.5 22.0 %copy.16 = bf16[1,1152,2176]{2,1,0:T(8,128)(2,1)} copy(bf16[1,1152,2176]{1,0,2:T(2,128)(2,1)} %all-gather.6.cloned.1.call-done) | data formatting | bytes 10027008 | tf_op jit(solution)/shard_map/all_gather | solution.py:74
  521.5 213.1 %while.14 = (s32[]{:T(128)}, bf16[64,1152]{1,0:T(8,128)(2,1)S(1)}, s32[]{:T(128)}, pred[]{:T(512)}, bf16[8,64,1152]{2,1,0:T(8,128)(2,1)}, /*index=5*/bf16[1152,2...) while((s32[]{:T(128)}, bf16[64,1152]{1,0:T(8,128)(2,1)S(1)}, ...), condition=%wide.region_5.6_spmd, body=%wide.region_0.5_spmd.sunk | while | flops 644014144 | bytes 11946512 | solution.py:94
  522.5 6.1 conditional.2
  522.9 5.7 fusion
  528.6 1.9 collective-permute-start
  530.5 7.3 collective-permute-done
  538.7 6.1 conditional.2
  539.1 5.7 fusion
  544.8 1.9 collective-permute-start
  546.7 6.1 collective-permute-done
  553.7 6.1 conditional.2
  554.1 5.7 fusion
  561.7 6.1 collective-permute-done
  568.7 6.1 conditional.2
  569.1 5.7 fusion
  576.7 6.1 collective-permute-done
  583.7 6.1 conditional.2
  584.1 5.7 fusion
  589.8 1.9 collective-permute-start
  591.8 6.1 collective-permute-done
  598.8 6.1 conditional.2
  599.1 5.7 fusion
  604.9 1.9 collective-permute-start
  606.8 6.1 collective-permute-done
  613.8 6.1 conditional.2
  614.2 5.7 fusion
  621.8 6.1 collective-permute-done
  628.8 6.1 conditional.2
  629.2 5.7 fusion
  636.8 6.1 collective-permute-done
  643.8 5.9 collective-permute-start
  649.7 4.2 collective-permute-done
  656.8 10.0 collective-permute-done
  669.7 10.0 collective-permute-done
  682.6 10.0 collective-permute-done
  693.6 1.9 collective-permute-start
  695.5 11.4 collective-permute-done
  709.9 11.8 collective-permute-done
  724.5 10.1 collective-permute-done
  736.0 22.1 %all-gather = bf16[8,9,1152]{2,1,0:T(8,128)(2,1)S(1)} all-gather(bf16[1,9,1152]{2,1,0:T(8,128)(2,1)S(1)} %maximum_bitcast_fusion), channel_id=1, replica_groups=mesh['pipe'=8,'dp'=64] {'pipe'}, dimensions={0}, use_global_device_ids=true | all-gather | bytes 186624 | tf_op jit(solution)/shard_map/all_gather | solution.py:104
  760.0 2.1 fusion.36
  765.9 91.5 %all-reduce.5.cloned.1.call-done = bf16[72,1152]{1,0:T(8,128)(2,1)} async-done(((bf16[72,1152]{1,0:T(8,128)(2,1)}), bf16[72,1152]{1,0:T(8,128)(2,1)}) %all-reduce.5.cloned.1.call-update) | async-done | bytes 165904
  858.8 529.3 %all-reduce.7.cloned.1.call-done = f32[576,1152]{1,0:T(8,128)} async-done(((f32[576,1152]{1,0:T(8,128)}), f32[576,1152]{1,0:T(8,128)}) %all-reduce.7.cloned.1.call-update) | async-done | bytes 2654224
  (106 shorter events, 50.9 us)
Async XLA Ops:
  7.2 155.3 %all-gather.10.cloned.1.call-start = ((), (), s32[]{:S(2)}) async-start(), calls=%async_computation.2 | async-start | bytes 2396160 | tf_op jit(solution)/shard_map/all_gather | solution.py:103
  9.6 321.1 %all-gather.8.cloned.1.call-start = ((), (), s32[]{:S(2)}) async-start(), calls=%async_computation.1 | async-start | bytes 10183680 | tf_op jit(solution)/shard_map/all_gather | solution.py:75
  11.4 488.1 %all-gather.6.cloned.1.call-start = ((), (), s32[]{:S(2)}) async-start(), calls=%async_computation | async-start | bytes 10183680 | tf_op jit(solution)/shard_map/all_gather | solution.py:74
  13.1 844.3 %all-reduce.5.cloned.1.call-start = ((), (), s32[]{:S(2)}) async-start(), calls=%async_computation.3 | async-start | bytes 331776
  528.6 9.2 collective-permute-start
  544.8 8.0 collective-permute-start
  559.8 8.0 collective-permute-start
  574.8 8.0 collective-permute-start
  589.8 8.0 collective-permute-start
  604.9 8.0 collective-permute-start
  619.9 8.0 collective-permute-start
  634.9 8.0 collective-permute-start
  643.8 10.1 collective-permute-start
  654.9 12.0 collective-permute-start
  667.8 12.0 collective-permute-start
  680.7 12.0 collective-permute-start
  693.6 13.4 collective-permute-start
  707.9 13.7 collective-permute-start
  722.6 12.0 collective-permute-start
  759.9 628.2 %all-reduce.7.cloned.1.call-start = ((), (), s32[]{:S(2)}) async-start(), calls=%async_computation.4 | async-start | bytes 5308416
Sparse Core Ops, SparseCore 0:
  11.8 150.6 all-gather.9
  165.7 164.9 all-gather.7
  333.9 165.5 all-gather.5
  760.0 97.3 all-reduce.4
  860.4 527.6 all-reduce.6
where the time goes:
time: 1400 us
  waiting for transfers between devices  1210 us (86%)
  matrix products  49.4 us (4%)
  local copies, waits for them, and re-layouts  40.1 us (3%)
  starting transfers between devices  33 us (2%)
  other arithmetic  22.9 us (2%)
  blocking collectives  22.1 us (2%)
  between operations  17.1 us (1%)
    unnamed x7, waiting for transfers between devices  621 us
    all_gather x1, waiting for transfers between devices, body(): lax.all_gather(narrowing_kernel, 'dp', axis=1, tiled=True)  166 us
    all_gather x1, waiting for transfers between devices, body(): lax.all_gather(widening_kernel, 'dp', axis=2, tiled=True)  162 us
    all_gather x1, waiting for transfers between devices, body(): text_row_block = lax.all_gather(caption_vectors, 'dp', axis=0, tiled=True)  145 us
    ppermute x15, waiting for transfers between devices, from_behind(): return lax.ppermute(value, axis, pairs)  117 us
    dot_general x8, matrix products, section_block(): jnp.dot(activated, w_down, preferred_element_type=jnp.float32)  45.6 us
    ppermute x15, starting transfers between devices, from_behind(): return lax.ppermute(value, axis, pairs)  32.8 us
  transfers between devices with their start and end apart: 20, of which 20 were waited for; matrix products, arithmetic and copies ran while one was open for 2% of the time, Pallas kernels for 0%

commit v1 on v0

--- a/solution.py
+++ b/solution.py
@@ -2,6 +2,13 @@
 import jax.numpy as jnp
 from jax import lax
 from jax.sharding import PartitionSpec as P
+
+
+def exchange_gather(block, mesh_axis, d):
+    size = lax.axis_size(mesh_axis)
+    blocks = jnp.stack([block for _ in range(size)])
+    blocks = lax.all_to_all(blocks, mesh_axis, split_axis=0, concat_axis=0)
+    return jnp.concatenate(blocks, axis=d)
 
 
 def from_behind(value, axis, steps):
@@ -71,7 +78,7 @@
     shift_addend = score_shift[0]
     caption_vectors = unit_rows(caption_outputs)
     up_full, down_full = (
-        lax.all_gather(widening_kernel, "dp", axis=2, tiled=True),
+        exchange_gather(widening_kernel, "dp", 2),
         lax.all_gather(narrowing_kernel, "dp", axis=1, tiled=True),
     )
     up_full = up_full[0]

time: 1400 us -> 1330 us (0.950)
  waiting for transfers between devices: 1210 us -> 1140 us
  starting transfers between devices: 33 us -> 53 us
    all_gather x1 -> x0, waiting for transfers between devices: 162 us -> none  [body(): lax.all_gather(widening_kernel, 'dp', axis=2, tiled=True)]
    all_gather x1, waiting for transfers between devices: 145 us -> 203 us  [body(): text_row_block = lax.all_gather(caption_vectors, 'dp', axis=0, tiled=True)]
    all_gather x1, waiting for transfers between devices: 166 us -> 195 us  [body(): lax.all_gather(narrowing_kernel, 'dp', axis=1, tiled=True)]
    all_gather x1 -> x0, local copies, waits for them, and re-layouts: 22 us -> none  [body(): lax.all_gather(widening_kernel, 'dp', axis=2, tiled=True)]
    all_to_all x0 -> x1, starting transfers between devices: none -> 20.1 us  [exchange_gather(): blocks = lax.all_to_all(blocks, mesh_axis, split_axis=0, concat_axis=0)]
    unnamed x7 -> x6, waiting for transfers between devices: 621 us -> 621 us
  transfers between devices with their start and end apart: 20 -> 20, of which waited for: 20 -> 19; matrix products, arithmetic and copies ran while one was open for 2% -> 1% of each run, Pallas kernels for 0% -> 0%
where the time goes in v1:
time: 1330 us
  waiting for transfers between devices  1140 us (86%)
  starting transfers between devices  53 us (4%)
  matrix products  49.4 us (4%)
  local copies, waits for them, and re-layouts  34.7 us (3%)
  blocking collectives  22.1 us (2%)
  other arithmetic  19.8 us (1%)
  between operations  17.2 us (1%)
    unnamed x6, waiting for transfers between devices  621 us
    all_gather x1, waiting for transfers between devices, body(): text_row_block = lax.all_gather(caption_vectors, 'dp', axis=0, tiled=True)  203 us
    all_gather x1, waiting for transfers between devices, body(): lax.all_gather(narrowing_kernel, 'dp', axis=1, tiled=True)  195 us
    ppermute x15, waiting for transfers between devices, from_behind(): return lax.ppermute(value, axis, pairs)  117 us
    dot_general x8, matrix products, section_block(): jnp.dot(activated, w_down, preferred_element_type=jnp.float32)  45.6 us
    ppermute x15, starting transfers between devices, from_behind(): return lax.ppermute(value, axis, pairs)  32.8 us
  transfers between devices with their start and end apart: 20, of which 19 were waited for; matrix products, arithmetic and copies ran while one was open for 1% of the time, Pallas kernels for 0%

profile of v1, /device:TPU:1, one launch (start us, length us, event | category | flops | bytes accessed | tf_op | source)
XLA Modules:
  0.0 1333.4 jit_solution(2036762031767396735)
XLA Ops:
  7.2 3.8 stack.2
  11.0 20.1 %all-to-all-start = ((bf16[64,1,1152,34]{2,3,1,0:T(8,128)(2,1)}), bf16[64,1,1152,34]{2,3,1,0:T(8,128)(2,1)}, u32[]{:S(2)}, u32[]{:S(2)}) async-start(bf16[64,1,1152,34]{2,3,1,0:T(8,128)(2,1)} %stack.2), calls=%async_computation | async-start | bytes 11796480 | tf_op jit(solution)/shard_map/all_to_all | solution.py:10
  34.6 203.2 %all-gather.7.cloned.1.call-done = bf16[64,9,1152]{2,1,0:T(8,128)(2,1)} async-done(((bf16[1,9,1152]{2,1,0:T(8,128)(2,1)}), bf16[64,9,1152]{2,1,0:T(8,128)(2,1)}) %all-gather.7.cloned.1.call-update) | async-done | bytes 1327120 | tf_op jit(solution)/shard_map/all_gather | solution.py:110
  237.9 2.6 reshape.86
  240.5 195.1 %all-gather.5.cloned.1.call-done = bf16[1,2176,1152]{2,0,1:T(2,128)(2,1)} async-done(((bf16[1,34,1152]{2,0,1:T(2,128)(2,1)}), bf16[1,2176,1152]{2,0,1:T(2,128)(2,1)}) %all-gather.5.cloned.1.call-update) | async-done | bytes 5013520 | tf_op jit(solution)/shard_map/all_gather | solution.py:82
  435.6 6.9 copy.18
  442.6 7.6 squeeze_reshape.3
  450.2 8.4 copy.15
  458.6 213.1 %while.14 = (s32[]{:T(128)}, bf16[64,1152]{1,0:T(8,128)(2,1)S(1)}, s32[]{:T(128)}, pred[]{:T(512)}, bf16[8,64,1152]{2,1,0:T(8,128)(2,1)}, /*index=5*/bf16[1152,2...) while((s32[]{:T(128)}, bf16[64,1152]{1,0:T(8,128)(2,1)S(1)}, ...), condition=%wide.region_5.6_spmd, body=%wide.region_0.5_spmd.sunk | while | flops 644014144 | bytes 11946512 | solution.py:101
  459.6 6.1 conditional.2
  460.0 5.7 fusion
  467.6 7.3 collective-permute-done
  475.8 6.1 conditional.2
  476.2 5.7 fusion
  483.9 6.1 collective-permute-done
  490.9 6.1 conditional.2
  491.2 5.7 fusion
  498.9 6.1 collective-permute-done
  505.9 6.1 conditional.2
  506.3 5.7 fusion
  513.9 6.1 collective-permute-done
  520.9 6.1 conditional.2
  521.3 5.7 fusion
  527.0 1.9 collective-permute-start
  528.9 6.1 collective-permute-done
  535.9 6.1 conditional.2
  536.3 5.7 fusion
  542.0 1.9 collective-permute-start
  543.9 6.1 collective-permute-done
  550.9 6.1 conditional.2
  551.3 5.7 fusion
  557.0 1.9 collective-permute-start
  558.9 6.1 collective-permute-done
  565.9 6.1 conditional.2
  566.3 5.7 fusion
  574.0 6.1 collective-permute-done
  581.0 5.9 collective-permute-start
  586.9 4.2 collective-permute-done
  593.9 10.0 collective-permute-done
  606.9 10.0 collective-permute-done
  619.8 10.0 collective-permute-done
  632.7 11.4 collective-permute-done
  647.0 11.8 collective-permute-done
  661.7 10.1 collective-permute-done
  673.2 22.1 %all-gather = bf16[8,9,1152]{2,1,0:T(8,128)(2,1)S(1)} all-gather(bf16[1,9,1152]{2,1,0:T(8,128)(2,1)S(1)} %maximum_bitcast_fusion), channel_id=1, replica_groups=mesh['pipe'=8,'dp'=64] {'pipe'}, dimensions={0}, use_global_device_ids=true | all-gather | bytes 186624 | tf_op jit(solution)/shard_map/all_gather | solution.py:111
  697.1 2.1 fusion.36
  703.0 91.5 %all-reduce.5.cloned.1.call-done = bf16[72,1152]{1,0:T(8,128)(2,1)} async-done(((bf16[72,1152]{1,0:T(8,128)(2,1)}), bf16[72,1152]{1,0:T(8,128)(2,1)}) %all-reduce.5.cloned.1.call-update) | async-done | bytes 165904
  796.0 529.3 %all-reduce.7.cloned.1.call-done = f32[576,1152]{1,0:T(8,128)} async-done(((f32[576,1152]{1,0:T(8,128)}), f32[576,1152]{1,0:T(8,128)}) %all-reduce.7.cloned.1.call-update) | async-done | bytes 2654224
  (114 shorter events, 48.3 us)
Async XLA Ops:
  10.9 20.2 %copy-start = (bf16[9,1152]{1,0:T(8,128)(2,1)S(1)}, bf16[9,1152]{1,0:T(8,128)(2,1)}, u32[]{:S(2)}) copy-start(bf16[9,1152]{1,0:T(8,128)(2,1)} %param.15) | copy-start | bytes 62212
  11.0 21.1 %copy-start.2 = (bf16[1,34,1152]{2,1,0:T(8,128)(2,1)S(1)}, bf16[1,34,1152]{2,1,0:T(8,128)(2,1)}, u32[]{:S(2)}) copy-start(bf16[1,34,1152]{2,1,0:T(8,128)(2,1)} %param.14) | copy-start | bytes 235012
  11.0 23.2 %copy-start.3 = (s32[4608]{0:T(1024)S(1)}, s32[4608]{0:T(1024)}, u32[]{:S(2)}) copy-start(s32[4608]{0:T(1024)} %param.17) | copy-start | bytes 55300
  11.0 23.5 %copy-start.1 = (f32[8,1152]{1,0:T(8,128)S(1)}, f32[8,1152]{1,0:T(8,128)}, u32[]{:S(2)}) copy-start(f32[8,1152]{1,0:T(8,128)} %param.16) | copy-start | bytes 110596
  11.0 431.6 %all-to-all-start = ((bf16[64,1,1152,34]{2,3,1,0:T(8,128)(2,1)}), bf16[64,1,1152,34]{2,3,1,0:T(8,128)(2,1)}, u32[]{:S(2)}, u32[]{:S(2)}) async-start(bf16[64,1,1152,34]{2,3,1,0:T(8,128)(2,1)} %stack.2), calls=%async_computation | async-start | bytes 11796480 | tf_op jit(solution)/shard_map/all_to_all | solution.py:10
  31.1 206.8 %all-gather.7.cloned.1.call-start = ((), (), s32[]{:S(2)}) async-start(), calls=%async_computation.2 | async-start | bytes 2396160 | tf_op jit(solution)/shard_map/all_gather | solution.py:110
  32.0 403.7 %all-gather.5.cloned.1.call-start = ((), (), s32[]{:S(2)}) async-start(), calls=%async_computation.1 | async-start | bytes 10183680 | tf_op jit(solution)/shard_map/all_gather | solution.py:82
  32.8 761.7 %all-reduce.5.cloned.1.call-start = ((), (), s32[]{:S(2)}) async-start(), calls=%async_computation.3 | async-start | bytes 331776
  465.7 9.2 collective-permute-start
  481.9 8.0 collective-permute-start
  496.9 8.0 collective-permute-start
  512.0 8.0 collective-permute-start
  527.0 8.0 collective-permute-start
  542.0 8.0 collective-permute-start
  557.0 8.0 collective-permute-start
  572.0 8.0 collective-permute-start
  581.0 10.1 collective-permute-start
  592.0 12.0 collective-permute-start
  604.9 12.0 collective-permute-start
  617.8 12.0 collective-permute-start
  630.8 13.4 %collective-permute-start = (bf16[64,1152]{1,0:T(8,128)(2,1)S(1)}, bf16[64,1152]{1,0:T(8,128)(2,1)S(1)}, u32[]{:S(2)}, u32[]{:S(2)}) collective-permute-start(bf16[64,1152]{1,0:T(8,128)(2,1)S(1)} %get-tuple-element.270), channel_id=1, source_target_pairs={{0,64},{64,128},{128,192},{192,256},{256,320},{320,384},{384,448},... | collective-permute-start | bytes 442376 | tf_op jit(solution)/shard_map/while/body/eval_jaxpr/ppermute | solution.py:17
  645.1 13.7 %collective-permute-start = (bf16[64,1152]{1,0:T(8,128)(2,1)S(1)}, bf16[64,1152]{1,0:T(8,128)(2,1)S(1)}, u32[]{:S(2)}, u32[]{:S(2)}) collective-permute-start(bf16[64,1152]{1,0:T(8,128)(2,1)S(1)} %get-tuple-element.270), channel_id=1, source_target_pairs={{0,64},{64,128},{128,192},{192,256},{256,320},{320,384},{384,448},... | collective-permute-start | bytes 442376 | tf_op jit(solution)/shard_map/while/body/eval_jaxpr/ppermute | solution.py:17
  659.7 12.0 collective-permute-start
  697.1 628.2 %all-reduce.7.cloned.1.call-start = ((), (), s32[]{:S(2)}) async-start(), calls=%async_computation.4 | async-start | bytes 5308416
Sparse Core Ops, SparseCore 0:
  35.7 202.1 all-gather.6
  241.0 194.5 all-gather.4
  697.2 97.2 all-reduce.4
  797.6 527.6 all-reduce.6
